TPU v7x, 256 devices: a whole 4x4x8 slice. The times are simulated.
256 devices in a mesh: tm: 8 (over y_hi, x), cells: 32 (over z, y_lo, core).
Axes of the slice: x: 4, y: 4 (y_hi: 2, y_lo: 2; y = y_hi * 2 + y_lo), z: 8, core: 2. Of those that a mesh axis runs over, the one named last changes fastest.
Arguments:
- footprint: float32 [8, 4, 768, 8192], P('tm', None, None, 'cells'), may hold values from -0.03125 to 0.03125
- flux: float32 [8, 8192, 2048], P('tm', 'cells'), may hold values from -6 to 6
- obs_weight: float32 [8, 768], P('tm'), may hold values from 0.2 to 5
- obs_count: int32 [8], P('tm'), may hold values from 1 to 768, 4608 in all
Outputs:
- normal_image: float32 [8, 8192, 2048], P('tm', 'cells')
Inputs may be any that keep to these rules, and one draw needn't show every extreme that they name: `obs_count`: each block has at least one valid slot; one block has all 768 slots valid.
All inputs are finite; a program needn't handle non-finite values.
Results may differ from a plain program's by a relative error of at most 0.0001.
Values sent between devices are 32-bit elements; how exact they have to be, the bound alone decides.
A program may use at most 128 MiB of HBM per device.

v0:
```python
import jax
import jax.numpy as jnp
from jax import lax
from jax.sharding import Mesh
from jax.sharding import PartitionSpec as P

CELLS = ("cells_0", "cells_1", "cells_2")


def from_behind(value, axis, by):
    devices = lax.axis_size(axis)
    pairs = [(i, i + by) for i in range(devices) if 0 <= i + by < devices]
    return lax.ppermute(value, axis, pairs)


def padded_to(lines, devices):
    spare = -lines.shape[0] % devices
    if not spare:
        return lines
    return jnp.concatenate([lines, jnp.zeros((spare, *lines.shape[1:]), lines.dtype)])


def nested_sum(value, near, far):
    lines = value.reshape(-1, *value.shape[1:][-1:])
    padded = padded_to(lines, lax.axis_size(near))
    own = lax.psum_scatter(padded, near, scatter_dimension=0, tiled=True)
    own = lax.psum(own, far)
    whole = lax.all_gather(own, near, axis=0, tiled=True)
    return whole[: len(lines)].reshape(value.shape)


def on_device(footprint, flux, obs_weight, obs_count):
    highest = lax.Precision.HIGHEST
    foot_slab = footprint[0]
    own_flux = flux[0]
    lag_count = foot_slab.shape[0]
    slot_count = foot_slab.shape[1]
    earlier = [own_flux]
    for lag_step in range(1, lag_count):
        earlier.append(from_behind(own_flux, "tm", lag_step))
    valid_rows = (jnp.arange(slot_count, dtype=jnp.int32) < obs_count[0]).astype(jnp.float32)
    row_scale = valid_rows * obs_weight[0]
    partial_value = jnp.dot(
        foot_slab[0], earlier[0], precision=highest, preferred_element_type=jnp.float32
    )
    for lag_step in range(1, lag_count):
        partial_value = partial_value + jnp.dot(
            foot_slab[lag_step],
            earlier[lag_step],
            precision=highest,
            preferred_element_type=jnp.float32,
        )
    modelled = nested_sum(partial_value, "cells_2", ("cells_0", "cells_1"))
    weighted = row_scale[:, None] * modelled
    adjoint_terms = []
    for lag_step in range(lag_count):
        adjoint_terms.append(
            lax.dot_general(
                foot_slab[lag_step],
                weighted,
                (((0,), (0,)), ((), ())),
                precision=highest,
                preferred_element_type=jnp.float32,
            )
        )
    accumulator = adjoint_terms[0]
    for lag_step in range(1, lag_count):
        accumulator = accumulator + from_behind(adjoint_terms[lag_step], "tm", -lag_step)
    return accumulator[None]


def solution(mesh):
    torus = Mesh(
        mesh.devices.reshape(mesh.shape["tm"], 8, 2, 2), ("tm", "cells_0", "cells_1", "cells_2")
    )
    placed = (P("tm", None, None, CELLS), P("tm", CELLS, None), P("tm", None), P("tm"))
    return jax.shard_map(
        on_device, mesh=torus, in_specs=placed, out_specs=P("tm", CELLS, None), check_vma=False
    )
```

profile of v0, /device:TPU:6, one launch (start us, length us, event | category | flops | bytes accessed | tf_op | source)
XLA Modules:
  0.0 543.6 jit_solution(7691611369154677838)
XLA Ops:
  6.5 6.2 %collective-permute-start.1 = (f32[256,2048]{1,0:T(8,128)}, f32[256,2048]{1,0:T(8,128)S(1)}, u32[]{:S(2)}, u32[]{:S(2)}) collective-permute-start(f32[256,2048]{1,0:T(8,128)} %bitcast.48), channel_id=1, source_target_pairs={{0,64},{32,96},{64,128},{96,160},{128,192},{160,224},{1,65},{33,97... | collective-permute-start | bytes 6291464 | tf_op jit(solution)/shard_map/ppermute | solution.py:13
  12.7 4.0 collective-permute-start
  16.8 1.9 collective-permute-start.2
  18.7 7.0 %fusion.48 = f32[768,2048]{1,0:T(8,128)S(1)} fusion(f32[1,4,768,256]{3,2,1,0:T(8,128)} %param.4, f32[1,256,2048]{2,1,0:T(8,128)} %param.5), kind=kOutput, calls=%fused_computation.31 | convolution fusion | flops 4831838208 | bytes 9175040 | tf_op jit(solution)/shard_map/dot_general | solution.py:43
  25.7 33.4 %collective-permute-done.1 = f32[256,2048]{1,0:T(8,128)S(1)} collective-permute-done((f32[256,2048]{1,0:T(8,128)}, f32[256,2048]{1,0:T(8,128)S(1)}, u32[]{:S(2)}, u32[]{:S(2)}) %collective-permute-start.1) | collective-permute-done | bytes 2097184 | tf_op jit(solution)/shard_map/ppermute | solution.py:13
  59.1 5.1 fusion.42
  64.3 68.4 %collective-permute-done = f32[256,2048]{1,0:T(8,128)S(1)} collective-permute-done((f32[256,2048]{1,0:T(8,128)}, f32[256,2048]{1,0:T(8,128)S(1)}, u32[]{:S(2)}, u32[]{:S(2)}) %collective-permute-start) | collective-permute-done | bytes 2097184 | tf_op jit(solution)/shard_map/ppermute | solution.py:13
  132.7 5.3 fusion.45
  138.0 7.8 %add_add_fusion = f32[768,2048]{1,0:T(8,128)} fusion(f32[768,2048]{1,0:T(8,128)S(1)} %fusion.42, f32[768,2048]{1,0:T(8,128)S(1)} %fusion.48, f32[768,2048]{1,0:T(8,128)S(1)} %fusion.45, f32[256,2048]{1,0:T(8,128)S(1)} %collective-permute-done.2, f32[1,4,768,256]{3,2,1,0:T(8,128)S(1)} %copy-done.1), kind=kOutput, calls=%fused_computation | convolution fusion | flops 4836556800 | bytes 28049408 | tf_op jit(solution)/shard_map/dot_general | solution.py:47
  145.9 0.0 all-reduce.2.cloned.1.call-start
  145.9 32.8 %reduce-scatter.2.cloned.1.call-done = f32[384,2048]{1,0:T(8,128)} async-done(((f32[768,2048]{1,0:T(8,128)}), f32[384,2048]{1,0:T(8,128)}) %reduce-scatter.2.cloned.1.call-update) | async-done | bytes 3145744 | tf_op jit(solution)/shard_map/reduce_scatter | solution.py:26
  178.7 0.0 all-gather.2.cloned.1.call-start
  178.8 166.7 %all-reduce.2.cloned.1.call-done = f32[384,2048]{1,0:T(8,128)} async-done(((f32[384,2048]{1,0:T(8,128)}), f32[384,2048]{1,0:T(8,128)}) %all-reduce.2.cloned.1.call-update) | async-done | bytes 3145744 | tf_op jit(solution)/shard_map/psum | solution.py:27
  346.2 20.5 %all-gather.2.cloned.1.call-done = f32[768,2048]{1,0:T(8,128)} async-done(((f32[384,2048]{1,0:T(8,128)}), f32[768,2048]{1,0:T(8,128)}) %all-gather.2.cloned.1.call-update) | async-done | bytes 6291472 | tf_op jit(solution)/shard_map/all_gather | solution.py:28
  366.7 12.4 %fusion.15 = f32[256,2048]{0,1:T(8,128)S(1)} fusion(f32[768,2048]{1,0:T(8,128)} %all-gather.2.cloned.1.call-done, f32[768]{0:T(1024)S(1)} %fusion.58, f32[1,4,768,256]{3,2,1,0:T(8,128)S(1)} %copy-done.1), kind=kOutput, calls=%fused_computation.14 | convolution fusion | flops 4833411072 | bytes 9179136 | tf_op jit(solution)/shard_map/dot_general | solution.py:58
  379.2 3.0 collective-permute-start.3
  382.1 10.4 %fusion.18 = f32[256,2048]{0,1:T(8,128)S(1)} fusion(f32[768,2048]{1,0:T(8,128)S(1)} %copy-done, f32[768]{0:T(1024)S(1)} %fusion.58, f32[1,4,768,256]{3,2,1,0:T(8,128)S(1)} %copy-done.1), kind=kOutput, calls=%fused_computation.15 | convolution fusion | flops 4833411072 | bytes 9179136 | tf_op jit(solution)/shard_map/dot_general | solution.py:58
  392.6 3.7 collective-permute-start.4
  396.3 10.4 %fusion.21 = f32[256,2048]{0,1:T(8,128)S(1)} fusion(f32[768,2048]{1,0:T(8,128)S(1)} %copy-done, f32[768]{0:T(1024)S(1)} %fusion.58, f32[1,4,768,256]{3,2,1,0:T(8,128)S(1)} %copy-done.1), kind=kOutput, calls=%fused_computation.16 | convolution fusion | flops 4833411072 | bytes 9179136 | tf_op jit(solution)/shard_map/dot_general | solution.py:58
  406.8 2.1 collective-permute-start.5
  408.9 88.0 %collective-permute-done.3 = f32[256,2048]{0,1:T(8,128)S(1)} collective-permute-done((f32[256,2048]{0,1:T(8,128)S(1)}, f32[256,2048]{0,1:T(8,128)S(1)}, u32[]{:S(2)}, u32[]{:S(2)}) %collective-permute-start.3) | collective-permute-done | bytes 2097184 | tf_op jit(solution)/shard_map/ppermute | solution.py:13
  496.9 25.5 %collective-permute-done.5 = f32[256,2048]{0,1:T(8,128)S(1)} collective-permute-done((f32[256,2048]{0,1:T(8,128)S(1)}, f32[256,2048]{0,1:T(8,128)S(1)}, u32[]{:S(2)}, u32[]{:S(2)}) %collective-permute-start.5) | collective-permute-done | bytes 2097184 | tf_op jit(solution)/shard_map/ppermute | solution.py:13
  522.4 11.7 %fusion.33 = f32[1,256,2048]{1,2,0:T(8,128)} fusion(f32[256,2048]{0,1:T(8,128)S(1)} %collective-permute-done.5, f32[256,2048]{0,1:T(8,128)S(1)} %collective-permute-done.4, f32[256,2048]{0,1:T(8,128)S(1)} %collective-permute-done.3, f32[768,2048]{1,0:T(8,128)S(1)} %copy-done, f32[768]{0:T(1024)S(1)} %fusion.58, f32[1,4,768,256]{3,2,1,0:T(8,128)S(1)} %copy-done.1), kind=kOutput, calls=%fused_computation.20 | convolution fusion | flops 4834983936 | bytes 15470592 | tf_op jit(solution)/shard_map/dot_general | solution.py:58
  534.0 2.9 copy.5
  (14 shorter events, 0.1 us)
Async XLA Ops:
  6.5 172.2 %reduce-scatter.2.cloned.1.call-start = ((), (), s32[]{:S(2)}) async-start(), calls=%async_computation.1 | async-start | bytes 9437184 | tf_op jit(solution)/shard_map/reduce_scatter | solution.py:26
  6.5 52.6 %copy-start.1 = (f32[1,4,768,256]{3,2,1,0:T(8,128)S(1)}, f32[1,4,768,256]{3,2,1,0:T(8,128)}, u32[]{:S(2)}) copy-start(f32[1,4,768,256]{3,2,1,0:T(8,128)} %param.4) | copy-start | bytes 9437188
  6.5 52.6 %collective-permute-start.1 = (f32[256,2048]{1,0:T(8,128)}, f32[256,2048]{1,0:T(8,128)S(1)}, u32[]{:S(2)}, u32[]{:S(2)}) collective-permute-start(f32[256,2048]{1,0:T(8,128)} %bitcast.48), channel_id=1, source_target_pairs={{0,64},{32,96},{64,128},{96,160},{128,192},{160,224},{1,65},{33,97... | collective-permute-start | bytes 6291464 | tf_op jit(solution)/shard_map/ppermute | solution.py:13
  12.7 119.9 %collective-permute-start = (f32[256,2048]{1,0:T(8,128)}, f32[256,2048]{1,0:T(8,128)S(1)}, u32[]{:S(2)}, u32[]{:S(2)}) collective-permute-start(f32[256,2048]{1,0:T(8,128)} %bitcast.49), channel_id=1, source_target_pairs={{0,32},{32,64},{64,96},{96,128},{128,160},{160,192},{192,224},{1,3... | collective-permute-start | bytes 6291464 | tf_op jit(solution)/shard_map/ppermute | solution.py:13
  16.8 121.3 %collective-permute-start.2 = (f32[256,2048]{1,0:T(8,128)}, f32[256,2048]{1,0:T(8,128)S(1)}, u32[]{:S(2)}, u32[]{:S(2)}) collective-permute-start(f32[256,2048]{1,0:T(8,128)} %bitcast.50), channel_id=1, source_target_pairs={{0,96},{32,128},{64,160},{96,192},{128,224},{1,97},{33,129},{65,16... | collective-permute-start | bytes 6291464 | tf_op jit(solution)/shard_map/ppermute | solution.py:13
  145.9 199.6 %all-reduce.2.cloned.1.call-start = ((), (), s32[]{:S(2)}) async-start(), calls=%async_computation.2 | async-start | bytes 6291456 | tf_op jit(solution)/shard_map/psum | solution.py:27
  178.7 167.4 %copy-start.2 = (f32[1,768]{1,0:T(1,128)S(1)}, f32[1,768]{1,0:T(1,128)}, u32[]{:S(2)}) copy-start(f32[1,768]{1,0:T(1,128)} %param.6) | copy-start | bytes 9220
  178.7 188.0 %all-gather.2.cloned.1.call-start = ((), (), s32[]{:S(2)}) async-start(), calls=%async_computation.3 | async-start | bytes 9437184 | tf_op jit(solution)/shard_map/all_gather | solution.py:28
  366.7 15.4 %copy-start = (f32[768,2048]{1,0:T(8,128)S(1)}, f32[768,2048]{1,0:T(8,128)}, u32[]{:S(2)}) copy-start(f32[768,2048]{1,0:T(8,128)} %all-gather.2.cloned.1.call-done) | copy-start | bytes 18874372
  379.2 117.8 %collective-permute-start.3 = (f32[256,2048]{0,1:T(8,128)S(1)}, f32[256,2048]{0,1:T(8,128)S(1)}, u32[]{:S(2)}, u32[]{:S(2)}) collective-permute-start(f32[256,2048]{0,1:T(8,128)S(1)} %fusion.15), channel_id=1, source_target_pairs={{32,0},{64,32},{96,64},{128,96},{160,128},{192,160},{224,192},{33,... | collective-permute-start | bytes 6291464 | tf_op jit(solution)/shard_map/ppermute | solution.py:13
  392.6 104.3 %collective-permute-start.4 = (f32[256,2048]{0,1:T(8,128)S(1)}, f32[256,2048]{0,1:T(8,128)S(1)}, u32[]{:S(2)}, u32[]{:S(2)}) collective-permute-start(f32[256,2048]{0,1:T(8,128)S(1)} %fusion.18), channel_id=1, source_target_pairs={{64,0},{96,32},{128,64},{160,96},{192,128},{224,160},{65,1},{97,33... | collective-permute-start | bytes 6291464 | tf_op jit(solution)/shard_map/ppermute | solution.py:13
  406.8 115.6 %collective-permute-start.5 = (f32[256,2048]{0,1:T(8,128)S(1)}, f32[256,2048]{0,1:T(8,128)S(1)}, u32[]{:S(2)}, u32[]{:S(2)}) collective-permute-start(f32[256,2048]{0,1:T(8,128)S(1)} %fusion.21), channel_id=1, source_target_pairs={{96,0},{128,32},{160,64},{192,96},{224,128},{97,1},{129,33},{161,6... | collective-permute-start | bytes 6291464 | tf_op jit(solution)/shard_map/ppermute | solution.py:13
Sparse Core Ops, SparseCore 0:
  146.0 32.6 reduce-scatter.1
  181.4 164.0 all-reduce.1
  347.2 19.4 all-gather.1
where the time goes:
time: 553 us; the launch traced here: 544 us
  waiting for transfers between devices  435 us (79%)
  matrix products  70.3 us (13%)
  starting transfers between devices  21 us (4%)
  between operations  14.1 us (3%)
    ppermute x6, waiting for transfers between devices, from_behind(): return lax.ppermute(value, axis, pairs)  215 us
    psum x1, waiting for transfers between devices, nested_sum(): own = lax.psum(own, far)  167 us
    dot_general x4, matrix products, on_device(): lax.dot_general(foot_slab[lag_step], weighted, (((0,), (0,)), ((), ())),...  45 us
    reduce_scatter x1, waiting for transfers between devices, nested_sum(): own = lax.psum_scatter(padded, near, scatter_dimension=0, tiled=True)  32.8 us
    ppermute x6, starting transfers between devices, from_behind(): return lax.ppermute(value, axis, pairs)  20.9 us
    all_gather x1, waiting for transfers between devices, nested_sum(): whole = lax.all_gather(own, near, axis=0, tiled=True)  20.5 us
    dot_general x3, matrix products, on_device(): jnp.dot(foot_slab[lag_step], earlier[lag_step], precision=highest, prefer...  18.3 us
  transfers between devices with their start and end apart: 9, of which 7 were waited for; matrix products, arithmetic and copies ran while one was open for 7% of the time, Pallas kernels for 0%

commit v1 on v0

--- a/solution.py
+++ b/solution.py
@@ -24,7 +24,7 @@
     lines = value.reshape(-1, *value.shape[1:][-1:])
     padded = padded_to(lines, lax.axis_size(near))
     own = lax.psum_scatter(padded, near, scatter_dimension=0, tiled=True)
-    own = lax.psum(own, far)
+    own = jnp.sum(lax.all_gather(own, far), axis=0)
     whole = lax.all_gather(own, near, axis=0, tiled=True)
     return whole[: len(lines)].reshape(value.shape)
 

time: 553 us -> 1440 us (2.60)
  waiting for transfers between devices: 435 us -> 1300 us
  other arithmetic: 0.02 us -> 18.8 us
    all_gather x0 -> x1, waiting for transfers between devices: none -> 1030 us  [nested_sum(): own = jnp.sum(lax.all_gather(own, far), axis=0)]
    psum x1 -> x0, waiting for transfers between devices: 167 us -> none  [nested_sum(): own = lax.psum(own, far)]
    reduce_sum x0 -> x1, other arithmetic: none -> 18.8 us  [nested_sum(): own = jnp.sum(lax.all_gather(own, far), axis=0)]
  transfers between devices with their start and end apart: 9 -> 9, of which waited for: 7 -> 7; matrix products, arithmetic and copies ran while one was open for 7% -> 3% of each run, Pallas kernels for 0% -> 0%
where the time goes in v1:
time: 1440 us; the launch traced here: 1430 us
  waiting for transfers between devices  1300 us (90%)
  matrix products  70.3 us (5%)
  starting transfers between devices  21 us (1%)
  other arithmetic  18.8 us (1%)
    all_gather x1, waiting for transfers between devices, nested_sum(): own = jnp.sum(lax.all_gather(own, far), axis=0)  1030 us
    ppermute x6, waiting for transfers between devices, from_behind(): return lax.ppermute(value, axis, pairs)  215 us
    dot_general x4, matrix products, on_device(): lax.dot_general(foot_slab[lag_step], weighted, (((0,), (0,)), ((), ())),...  45 us
    reduce_scatter x1, waiting for transfers between devices, nested_sum(): own = lax.psum_scatter(padded, near, scatter_dimension=0, tiled=True)  32.8 us
  transfers between devices with their start and end apart: 9, of which 7 were waited for; matrix products, arithmetic and copies ran while one was open for 3% of the time, Pallas kernels for 0%

profile of v1, /device:TPU:6, one launch (start us, length us, event | category | flops | bytes accessed | tf_op | source)
XLA Modules:
  0.0 1425.8 jit_solution(5210181963360276627)
XLA Ops:
  6.5 6.2 collective-permute-start.1
  12.7 4.0 collective-permute-start
  16.8 1.9 collective-permute-start.2
  18.7 7.0 fusion.48
  25.7 33.4 %collective-permute-done.1 = f32[256,2048]{1,0:T(8,128)S(1)} collective-permute-done((f32[256,2048]{1,0:T(8,128)}, f32[256,2048]{1,0:T(8,128)S(1)}, u32[]{:S(2)}, u32[]{:S(2)}) %collective-permute-start.1) | collective-permute-done | bytes 2097184 | tf_op jit(solution)/shard_map/ppermute | solution.py:13
  59.1 5.1 fusion.42
  64.3 68.4 %collective-permute-done = f32[256,2048]{1,0:T(8,128)S(1)} collective-permute-done((f32[256,2048]{1,0:T(8,128)}, f32[256,2048]{1,0:T(8,128)S(1)}, u32[]{:S(2)}, u32[]{:S(2)}) %collective-permute-start) | collective-permute-done | bytes 2097184 | tf_op jit(solution)/shard_map/ppermute | solution.py:13
  132.7 5.3 fusion.45
  138.0 7.8 add_add_fusion
  145.9 0.0 all-gather.6.cloned.1.call-start
  145.9 32.8 %reduce-scatter.2.cloned.1.call-done = f32[384,2048]{1,0:T(8,128)} async-done(((f32[768,2048]{1,0:T(8,128)}), f32[384,2048]{1,0:T(8,128)}) %reduce-scatter.2.cloned.1.call-update) | async-done | bytes 3145744 | tf_op jit(solution)/shard_map/reduce_scatter | solution.py:26
  178.8 1028.1 %all-gather.6.cloned.1.call-done = f32[6144,2048]{1,0:T(8,128)} async-done(((f32[384,2048]{1,0:T(8,128)}), f32[6144,2048]{1,0:T(8,128)}) %all-gather.6.cloned.1.call-update) | async-done | bytes 50331664 | tf_op jit(solution)/shard_map/all_gather | solution.py:27
  1206.9 18.8 %reduce_sum.9 = f32[384,2048]{1,0:T(8,128)} reduce(f32[16,384,2048]{2,1,0:T(8,128)} %bitcast.49, f32[]{:T(128)} %constant.2.clone.1), dimensions={0}, to_apply=%region_1.0 | reduce | flops 11796480 | bytes 53477380 | tf_op jit(solution)/shard_map/reduce_sum | solution.py:27
  1226.4 22.5 %all-gather.4.cloned.1.call-done = f32[768,2048]{1,0:T(8,128)} async-done(((f32[384,2048]{1,0:T(8,128)}), f32[768,2048]{1,0:T(8,128)}) %all-gather.4.cloned.1.call-update) | async-done | bytes 6291472 | tf_op jit(solution)/shard_map/all_gather | solution.py:28
  1248.9 12.4 fusion.15
  1261.3 3.0 collective-permute-start.3
  1264.3 10.4 fusion.18
  1274.8 3.7 collective-permute-start.4
  1278.5 10.4 fusion.21
  1289.0 2.1 collective-permute-start.5
  1291.1 88.0 %collective-permute-done.3 = f32[256,2048]{0,1:T(8,128)S(1)} collective-permute-done((f32[256,2048]{0,1:T(8,128)S(1)}, f32[256,2048]{0,1:T(8,128)S(1)}, u32[]{:S(2)}, u32[]{:S(2)}) %collective-permute-start.3) | collective-permute-done | bytes 2097184 | tf_op jit(solution)/shard_map/ppermute | solution.py:13
  1379.1 25.5 %collective-permute-done.5 = f32[256,2048]{0,1:T(8,128)S(1)} collective-permute-done((f32[256,2048]{0,1:T(8,128)S(1)}, f32[256,2048]{0,1:T(8,128)S(1)}, u32[]{:S(2)}, u32[]{:S(2)}) %collective-permute-start.5) | collective-permute-done | bytes 2097184 | tf_op jit(solution)/shard_map/ppermute | solution.py:13
  1404.6 11.7 fusion.33
  1416.2 2.9 copy.5
  (15 shorter events, 0.1 us)
Async XLA Ops:
  6.5 172.2 %reduce-scatter.2.cloned.1.call-start = ((), (), s32[]{:S(2)}) async-start(), calls=%async_computation.1 | async-start | bytes 9437184 | tf_op jit(solution)/shard_map/reduce_scatter | solution.py:26
  6.5 52.6 %copy-start.1 = (f32[1,4,768,256]{3,2,1,0:T(8,128)S(1)}, f32[1,4,768,256]{3,2,1,0:T(8,128)}, u32[]{:S(2)}) copy-start(f32[1,4,768,256]{3,2,1,0:T(8,128)} %param.4) | copy-start | bytes 9437188
  6.5 52.6 %collective-permute-start.1 = (f32[256,2048]{1,0:T(8,128)}, f32[256,2048]{1,0:T(8,128)S(1)}, u32[]{:S(2)}, u32[]{:S(2)}) collective-permute-start(f32[256,2048]{1,0:T(8,128)} %bitcast.50), channel_id=1, source_target_pairs={{0,64},{32,96},{64,128},{96,160},{128,192},{160,224},{1,65},{33,97... | collective-permute-start | bytes 6291464 | tf_op jit(solution)/shard_map/ppermute | solution.py:13
  12.7 119.9 %collective-permute-start = (f32[256,2048]{1,0:T(8,128)}, f32[256,2048]{1,0:T(8,128)S(1)}, u32[]{:S(2)}, u32[]{:S(2)}) collective-permute-start(f32[256,2048]{1,0:T(8,128)} %bitcast.51), channel_id=1, source_target_pairs={{0,32},{32,64},{64,96},{96,128},{128,160},{160,192},{192,224},{1,3... | collective-permute-start | bytes 6291464 | tf_op jit(solution)/shard_map/ppermute | solution.py:13
  16.8 121.3 %collective-permute-start.2 = (f32[256,2048]{1,0:T(8,128)}, f32[256,2048]{1,0:T(8,128)S(1)}, u32[]{:S(2)}, u32[]{:S(2)}) collective-permute-start(f32[256,2048]{1,0:T(8,128)} %bitcast.52), channel_id=1, source_target_pairs={{0,96},{32,128},{64,160},{96,192},{128,224},{1,97},{33,129},{65,16... | collective-permute-start | bytes 6291464 | tf_op jit(solution)/shard_map/ppermute | solution.py:13
  145.9 1061.0 %all-gather.6.cloned.1.call-start = ((), (), s32[]{:S(2)}) async-start(), calls=%async_computation.3 | async-start | bytes 53477376 | tf_op jit(solution)/shard_map/all_gather | solution.py:27
  178.7 1070.2 %all-gather.4.cloned.1.call-start = ((), (), s32[]{:S(2)}) async-start(), calls=%async_computation.2 | async-start | bytes 9437184 | tf_op jit(solution)/shard_map/all_gather | solution.py:28
  1225.7 0.7 copy-start.2
  1248.9 15.4 %copy-start = (f32[768,2048]{1,0:T(8,128)S(1)}, f32[768,2048]{1,0:T(8,128)}, u32[]{:S(2)}) copy-start(f32[768,2048]{1,0:T(8,128)} %all-gather.4.cloned.1.call-done) | copy-start | bytes 18874372
  1261.3 117.8 %collective-permute-start.3 = (f32[256,2048]{0,1:T(8,128)S(1)}, f32[256,2048]{0,1:T(8,128)S(1)}, u32[]{:S(2)}, u32[]{:S(2)}) collective-permute-start(f32[256,2048]{0,1:T(8,128)S(1)} %fusion.15), channel_id=1, source_target_pairs={{32,0},{64,32},{96,64},{128,96},{160,128},{192,160},{224,192},{33,... | collective-permute-start | bytes 6291464 | tf_op jit(solution)/shard_map/ppermute | solution.py:13
  1274.8 104.3 %collective-permute-start.4 = (f32[256,2048]{0,1:T(8,128)S(1)}, f32[256,2048]{0,1:T(8,128)S(1)}, u32[]{:S(2)}, u32[]{:S(2)}) collective-permute-start(f32[256,2048]{0,1:T(8,128)S(1)} %fusion.18), channel_id=1, source_target_pairs={{64,0},{96,32},{128,64},{160,96},{192,128},{224,160},{65,1},{97,33... | collective-permute-start | bytes 6291464 | tf_op jit(solution)/shard_map/ppermute | solution.py:13
  1289.0 115.6 %collective-permute-start.5 = (f32[256,2048]{0,1:T(8,128)S(1)}, f32[256,2048]{0,1:T(8,128)S(1)}, u32[]{:S(2)}, u32[]{:S(2)}) collective-permute-start(f32[256,2048]{0,1:T(8,128)S(1)} %fusion.21), channel_id=1, source_target_pairs={{96,0},{128,32},{160,64},{192,96},{224,128},{97,1},{129,33},{161,6... | collective-permute-start | bytes 6291464 | tf_op jit(solution)/shard_map/ppermute | solution.py:13
Sparse Core Ops, SparseCore 0:
  146.0 32.6 reduce-scatter.1
  180.5 1026.3 all-gather.5
  1225.9 22.9 all-gather.3
